TPU v7x, 512 devices: a whole 4x8x8 slice. The times are simulated.
512 devices in a mesh: pair: 16 (over z, core), virt: 32 (over x, y).
Axes of the slice: x: 4, y: 8, z: 8, core: 2. Of those that a mesh axis runs over, the one named last changes fastest.
Arguments:
- amplitudes: bfloat16 [1024, 512, 512], P('pair', 'virt')
- integrals: bfloat16 [8, 512, 512, 512], P(None, 'pair', 'virt')
- pair_occ: int32 [1024, 2], P('virt'), may hold values from 0 to 119, as said below
- occ_irrep: int32 [120], replicated, may hold values from 0 to 7, as said below
- virt_irrep: int32 [512], replicated, may hold values from 0 to 7, as said below
- occ_energy: float32 [120], replicated, may hold values from -3 to -0.5
- virt_energy: float32 [512], replicated, may hold values from 0.3 to 4
Outputs:
- update: float32 [1024, 8, 512], P('virt', None, 'pair')
Inputs may be any that keep to these rules, and one draw needn't show every extreme that they name: `pair_occ`: each row holds i < j, and rows are distinct. `occ_irrep`: labels of the D2h irreps; every label occurs. `virt_irrep`: labels of the D2h irreps; every label occurs.
All inputs are finite; a program needn't handle non-finite values.
Results may differ from a plain program's by a relative error of at most 0.0003.
Values may be sent and summed in bfloat16 or wider, within the bound.
A program may use at most 128 MiB of HBM per device.

v0:
```python
import jax
import jax.numpy as jnp
from jax import lax
from jax.sharding import PartitionSpec as P


def table_lookup(indices, table, zero_value):
    orbital = jnp.arange(table.shape[0], dtype=jnp.int32)
    hits = indices[:, None] == orbital[None, :]
    return jnp.sum(jnp.where(hits, table[None, :], zero_value), axis=1)


def local(amplitudes, integrals, pair_occ, occ_irrep, virt_irrep, occ_energy, virt_energy):
    window_size, local_width, local_depth, full_width = integrals.shape
    integral_matrix = integrals.reshape(window_size * local_width, local_depth * full_width)
    owned_rows = pair_occ.shape[0]
    block_rows = lax.all_gather(amplitudes, "pair", axis=0, tiled=True)
    flattened = block_rows.reshape(block_rows.shape[0], local_depth * full_width)
    partial_value = lax.dot_general(
        flattened, integral_matrix, (((1,), (1,)), ((), ())), preferred_element_type=jnp.float32
    )
    summed = lax.psum(partial_value, "virt")
    ladder = lax.dynamic_slice_in_dim(summed, lax.axis_index("virt") * owned_rows, owned_rows, 0)
    ladder = ladder.reshape(owned_rows, window_size, local_width)
    b_offset = lax.axis_index("pair") * local_width
    local_sym = lax.dynamic_slice_in_dim(virt_irrep, b_offset, local_width, 0)
    local_energy = lax.dynamic_slice_in_dim(virt_energy, b_offset, local_width, 0)
    first_occ = pair_occ[:, 0]
    second_occ = pair_occ[:, 1]
    pair_sym = jnp.bitwise_xor(
        table_lookup(first_occ, occ_irrep, 0), table_lookup(second_occ, occ_irrep, 0)
    )
    pair_energy = table_lookup(first_occ, occ_energy, 0.0) + table_lookup(
        second_occ, occ_energy, 0.0
    )
    window_sym = virt_irrep[:window_size]
    total_sym = jnp.bitwise_xor(
        pair_sym[:, None, None],
        jnp.bitwise_xor(window_sym[None, :, None], local_sym[None, None, :]),
    )
    allowed = total_sym == 0
    denom = (
        pair_energy[:, None, None]
        - virt_energy[:window_size][None, :, None]
        - local_energy[None, None, :]
    )
    return jnp.where(allowed, ladder / denom, jnp.zeros_like(ladder))


def solution(mesh):
    return jax.shard_map(
        local,
        mesh=mesh,
        in_specs=(
            P("pair", "virt", None),
            P(None, "pair", "virt", None),
            P("virt", None),
            P(),
            P(),
            P(),
            P(),
        ),
        out_specs=P("virt", None, "pair"),
        check_vma=False,
    )
```

profile of v0, /device:TPU:64, one launch (start us, length us, event | category | flops | bytes accessed | tf_op | source)
XLA Modules:
  0.0 301.6 jit_solution(1929621240613633479)
XLA Ops:
  6.5 0.7 all-gather.2.cloned.1.call-update
  7.3 0.0 all-reduce.2.cloned.1.call-start
  7.3 8.4 %copy.9 = bf16[32,8,16,512]{3,1,2,0:T(8,128)(2,1)} copy(bf16[32,8,16,512]{3,2,1,0:T(8,128)(2,1)} %bitcast.13) | data formatting | bytes 8388608
  15.7 94.0 %all-gather.2.cloned.1.call-done = bf16[1024,16,512]{2,1,0:T(8,128)(2,1)} async-done(((bf16[64,16,512]{2,1,0:T(8,128)(2,1)}), bf16[1024,16,512]{2,1,0:T(8,128)(2,1)}) %all-gather.2.cloned.1.call-update) | async-done | bytes 16777232 | tf_op jit(solution)/shard_map/all_gather | solution.py:17
  109.7 16.0 %copy.8 = bf16[128,8,16,512]{3,1,2,0:T(8,128)(2,1)S(1)} copy(bf16[128,8,16,512]{3,2,1,0:T(8,128)(2,1)} %bitcast.11) | data formatting | bytes 33554432
  125.7 0.0 copy-start.4
  125.7 0.0 copy-start.5
  125.7 0.0 copy-start.1
  125.8 0.0 copy-start.2
  125.8 0.0 copy-start.3
  125.8 0.0 slice-start.1
  125.8 0.0 slice-start
  125.8 5.5 %fusion = f32[1024,256]{1,0:T(8,128)} fusion(bf16[1024,8192]{1,0:T(8,128)(2,1)S(1)} %bitcast.12, bf16[256,8192]{1,0:T(8,128)(2,1)S(1)} %bitcast.14), kind=kOutput, calls=%fused_computation.13 | convolution fusion | flops 4294967296 | bytes 22020096 | tf_op jit(solution)/shard_map/dot_general | solution.py:19
  131.4 0.0 all-reduce.2.cloned.1.call-update
  131.4 0.1 dynamic_slice.11
  131.5 0.1 dynamic_slice.9
  131.6 0.2 select_reduce_fusion
  131.8 0.2 select_reduce_fusion.2
  132.0 0.1 broadcast_xor_fusion
  132.0 0.1 broadcast_subtract_fusion
  132.1 161.0 %all-reduce.2.cloned.1.call-done = f32[1024,256]{1,0:T(8,128)} async-done(((f32[1024,256]{1,0:T(8,128)}), f32[1024,256]{1,0:T(8,128)}) %all-reduce.2.cloned.1.call-update) | async-done | bytes 1048592 | tf_op jit(solution)/shard_map/psum | solution.py:22
  293.1 0.8 constant_dynamic-slice_fusion
  293.9 0.1 reshape.87
  294.0 0.8 divide_select_fusion
  (13 shorter events, 0.0 us)
Async XLA Ops:
  6.5 103.2 %all-gather.2.cloned.1.call-start = ((), (), s32[]{:S(2)}) async-start(), calls=%async_computation | async-start | bytes 17825792 | tf_op jit(solution)/shard_map/all_gather | solution.py:17
  7.3 285.9 %all-reduce.2.cloned.1.call-start = ((), (), s32[]{:S(2)}) async-start(), calls=%async_computation.1 | async-start | bytes 2097152 | tf_op jit(solution)/shard_map/psum | solution.py:22
  109.7 16.1 %copy-start = (bf16[32,8,16,512]{3,1,2,0:T(8,128)(2,1)S(1)}, bf16[32,8,16,512]{3,1,2,0:T(8,128)(2,1)}, u32[]{:S(2)}) copy-start(bf16[32,8,16,512]{3,1,2,0:T(8,128)(2,1)} %copy.9) | copy-start | bytes 12582916
  125.7 5.7 %copy-start.4 = (f32[512]{0:T(512)S(1)}, f32[512]{0:T(512)}, u32[]{:S(2)}) copy-start(f32[512]{0:T(512)} %param.13) | copy-start | bytes 6148
  125.7 5.7 %copy-start.5 = (s32[512]{0:T(512)S(1)}, s32[512]{0:T(512)}, u32[]{:S(2)}) copy-start(s32[512]{0:T(512)} %param.11) | copy-start | bytes 6148
  125.7 5.8 %copy-start.1 = (s32[32,2]{0,1:T(2,128)S(1)}, s32[32,2]{0,1:T(2,128)}, u32[]{:S(2)}) copy-start(s32[32,2]{0,1:T(2,128)} %param.9) | copy-start | bytes 772
  125.8 5.8 %copy-start.2 = (f32[120]{0:T(128)S(1)}, f32[120]{0:T(128)}, u32[]{:S(2)}) copy-start(f32[120]{0:T(128)} %param.12) | copy-start | bytes 1444
  125.8 6.0 %copy-start.3 = (s32[120]{0:T(128)S(1)}, s32[120]{0:T(128)}, u32[]{:S(2)}) copy-start(s32[120]{0:T(128)} %param.10) | copy-start | bytes 1444
  125.8 6.2 %slice-start.1 = ((s32[512]{0:T(512)}), s32[8]{0:T(128)S(1)}, s32[]{:S(2)}) async-start(s32[512]{0:T(512)} %param.11), calls=%async_computation.3 | async-start | bytes 1024 | tf_op jit(solution)/shard_map/slice | solution.py:36
  125.8 6.2 %slice-start = ((f32[512]{0:T(512)}), f32[8]{0:T(128)S(1)}, s32[]{:S(2)}) async-start(f32[512]{0:T(512)} %param.13), calls=%async_computation.2 | async-start | bytes 1024 | tf_op jit(solution)/shard_map/slice | solution.py:44
Sparse Core Ops, SparseCore 0:
  9.4 100.2 all-gather.1
  131.5 161.6 all-reduce.1
where the time goes:
time: 302 us
  waiting for transfers between devices  256 us (85%)
  local copies, waits for them, and re-layouts  25.5 us (8%)
  between operations  13.5 us (4%)
  matrix products  5.53 us (2%)
    psum x1, waiting for transfers between devices, local(): summed = lax.psum(partial_value, 'virt')  161 us
    all_gather x1, waiting for transfers between devices, local(): block_rows = lax.all_gather(amplitudes, 'pair', axis=0, tiled=True)  94 us
    unnamed x14, local copies, waits for them, and re-layouts  24.5 us
  transfers between devices with their start and end apart: 2, of which 2 were waited for; matrix products, arithmetic and copies ran while one was open for 3% of the time, Pallas kernels for 0%

commit v1 on v0

--- a/solution.py
+++ b/solution.py
@@ -1,7 +1,408 @@
+import functools
+
 import jax
 import jax.numpy as jnp
 from jax import lax
+from jax.experimental import pallas as pl
+from jax.experimental.pallas import tpu as pltpu
 from jax.sharding import PartitionSpec as P
+
+MESH = pl.DeviceIdType.MESH
+F32 = jnp.float32
+BF16 = jnp.bfloat16
+
+IRREPS = 8
+LANES = 128
+ROWS = 96
+CLASS_ROW = ROWS - 1
+OUT_SLOTS = 64
+CORES = 2
+
+
+def iota(shape, dim):
+    return lax.broadcasted_iota(jnp.int32, shape, dim)
+
+
+def mm(a, b):
+    return lax.dot_general(a, b, (((1,), (0,)), ((), ())), preferred_element_type=F32)
+
+
+def split3(x):
+    hi = x.astype(BF16)
+    rest = x - hi.astype(F32)
+    mid = rest.astype(BF16)
+    return hi, mid, (rest - mid.astype(F32)).astype(BF16)
+
+
+def select_dot(sel, x):
+    n = x.shape[1]
+    both = mm(sel, jnp.concatenate(split3(x), axis=1))
+    return (both[:, 2 * n :] + both[:, n : 2 * n]) + both[:, :n]
+
+
+def fold_kernel(
+    chips,
+    virts,
+    t_hbm,
+    v_hbm,
+    po_ref,
+    oi_ref,
+    vi_ref,
+    oe_ref,
+    ve_ref,
+    out_ref,
+    t_buf,
+    v_buf,
+    small,
+    slot_sel,
+    group_sel,
+    t_folded,
+    t_seen,
+    v_folded,
+    v_mat,
+    cls_ref,
+    fold_sel,
+    own,
+    sib,
+    stage,
+    recv,
+    local_sem,
+    ring_send,
+    ring_recv,
+    sib_send,
+    sib_recv,
+    piece_send,
+    piece_recv,
+):
+    pairs, depth, width = t_buf.shape
+    window, bwidth = v_buf.shape[0], v_buf.shape[1]
+    abs_ = window * bwidth
+    half_c = depth // 2
+    chunk = half_c // 2
+
+    pair = lax.axis_index("pair")
+    virt = lax.axis_index("virt")
+    z = lax.div(pair, CORES)
+    core = lax.rem(pair, CORES)
+    up = lax.rem(z + 1, chips) * CORES + core
+    down = lax.rem(z + chips - 1, chips) * CORES + core
+    other = z * CORES + (1 - core)
+
+    t_copy = pltpu.make_async_copy(t_hbm, t_buf, local_sem.at[0])
+    v_copy = pltpu.make_async_copy(v_hbm, v_buf, local_sem.at[1])
+    t_copy.start()
+    v_copy.start()
+
+    barrier = pltpu.get_barrier_semaphore()
+    for q in (up, down, other):
+        pl.semaphore_signal(barrier, inc=1, device_id={"pair": q}, device_id_type=MESH)
+
+    @pl.loop(1, virts)
+    def _(k):
+        w = lax.rem(virt + k, virts)
+        pl.semaphore_signal(barrier, inc=1, device_id={"virt": w}, device_id_type=MESH)
+
+    for blocks in (own, sib):
+        blocks[:, :, ROWS:, :] = jnp.zeros((chips, half_c, LANES - ROWS, LANES), BF16)
+
+    vi = vi_ref[...].astype(F32)
+    ve = ve_ref[...]
+    lane_d = iota((width, width), 1)
+    sub_d = iota((width, width), 0)
+    irr_col = jnp.sum(jnp.where(lane_d == sub_d, vi, 0.0), axis=1, keepdims=True)
+    lane_g = iota((width, LANES), 1)
+    hot = irr_col.astype(jnp.int32) == lane_g
+    hot_f = jnp.where(hot, 1.0, 0.0)
+    earlier = jnp.where(lane_d < sub_d, 1.0, 0.0).astype(BF16)
+    counts = mm(earlier, hot_f.astype(BF16))
+    slot = jnp.sum(jnp.where(hot, counts, 0.0), axis=1, keepdims=True)
+    slot_sel[...] = jnp.where(slot.astype(jnp.int32) == lane_g, 1.0, 0.0).astype(BF16)
+    group_sel[...] = hot_f.astype(BF16)
+
+    lane_c = iota((depth, width), 1)
+    sub_c = iota((depth, width), 0)
+    irr_c = jnp.sum(jnp.where(lane_c == virt * depth + sub_c, vi, 0.0), axis=1, keepdims=True)
+    lane_s = iota((depth, LANES), 1)
+    seen_class = jnp.where(
+        lane_s < IRREPS, jnp.bitwise_xor(irr_c.astype(jnp.int32), lane_s), 0
+    ).astype(F32)
+
+    lane_ab = iota((abs_, width), 1)
+    sub_ab = iota((abs_, width), 0)
+    sub_a = lax.div(sub_ab, bwidth)
+    hit_a = lane_ab == sub_a
+    hit_b = lane_ab == pair * bwidth + (sub_ab - sub_a * bwidth)
+    irr_a = jnp.sum(jnp.where(hit_a, vi, 0.0), axis=1, keepdims=True)
+    irr_b = jnp.sum(jnp.where(hit_b, vi, 0.0), axis=1, keepdims=True)
+    energy_a = jnp.sum(jnp.where(hit_a, ve, 0.0), axis=1, keepdims=True)
+    energy_b = jnp.sum(jnp.where(hit_b, ve, 0.0), axis=1, keepdims=True)
+    cls = jnp.bitwise_xor(irr_a.astype(jnp.int32), irr_b.astype(jnp.int32))
+    lane_k = iota((abs_, LANES), 1)
+    hot_ab = cls == lane_k
+    hot_ab_f = jnp.where(hot_ab, 1.0, 0.0)
+    before = jnp.where(iota((abs_, abs_), 1) < iota((abs_, abs_), 0), 1.0, 0.0).astype(BF16)
+    ranks = jnp.where(hot_ab, mm(before, hot_ab_f.astype(BF16)), 0.0)
+    rank = jnp.sum(ranks, axis=1, keepdims=True).astype(jnp.int32)
+    unfold_f = jnp.where(rank == lane_k, 1.0, 0.0)
+    unfold = unfold_f.astype(BF16)[:, :OUT_SLOTS]
+    fold_sel[...] = jnp.transpose(unfold_f)[:OUT_SLOTS, :].astype(BF16)
+    cls_ref[...] = jnp.broadcast_to(cls.astype(F32), (abs_, LANES))
+
+    t_copy.wait()
+    rows = pairs * depth
+    t_rows = t_buf[...].reshape(rows, width)
+    t_folded[...] = mm(t_rows, slot_sel[...])
+    live = jnp.where(t_rows.astype(F32) != 0.0, 1.0, 0.0).astype(BF16)
+    seen = mm(live, group_sel[...]).reshape(pairs, depth, LANES)
+    t_seen[...] = jnp.where(seen > 0.0, seen_class[None], 0.0).reshape(rows, LANES)
+    pair_cls = t_seen[pl.ds(0, pairs, stride=depth), :]
+    for c in range(1, depth):
+        pair_cls = jnp.maximum(pair_cls, t_seen[pl.ds(c, pairs, stride=depth), :])
+    pair_cls = jnp.max(pair_cls, axis=1, keepdims=True)
+
+    def fold_block(c2):
+        x = jnp.concatenate(
+            [
+                t_folded[pl.ds(c2, pairs, stride=depth), :],
+                t_folded[pl.ds(c2 + half_c, pairs, stride=depth), :],
+            ],
+            axis=0,
+        )
+        if c2 == 0:
+            label = jnp.concatenate([pair_cls, pair_cls], axis=0)
+            x = jnp.where(iota(x.shape, 1) == CLASS_ROW, label, x)
+        own[0, c2, :ROWS, :] = jnp.transpose(x)[:ROWS, :].astype(BF16)
+
+    def part(blocks, delta, ch):
+        return blocks.at[delta, pl.ds(ch * chunk, chunk), pl.ds(0, ROWS), :]
+
+    def ring_copy(way, d, ch):
+        src, dst = d - 1, d
+        if way == 0:
+            src, dst = (chips - src) % chips, (chips - dst) % chips
+        return pltpu.make_async_remote_copy(
+            src_ref=part(own, src, ch),
+            dst_ref=part(own, dst, ch),
+            send_sem=ring_send.at[way, d - 1, ch],
+            recv_sem=ring_recv.at[way, d - 1, ch],
+            device_id={"pair": up if way == 0 else down},
+            device_id_type=MESH,
+        )
+
+    def sib_copy(delta, ch):
+        return pltpu.make_async_remote_copy(
+            src_ref=part(own, delta, ch),
+            dst_ref=part(sib, delta, ch),
+            send_sem=sib_send.at[delta, ch],
+            recv_sem=sib_recv.at[delta, ch],
+            device_id={"pair": other},
+            device_id_type=MESH,
+        )
+
+    far = chips // 2
+
+    def travels(way, d, ch):
+        return d < far or (d == far and ch == way)
+
+    for c2 in range(chunk):
+        fold_block(c2)
+    pl.semaphore_wait(barrier, virts - 1 + 3)
+    ring_copy(0, 1, 0).start()
+    ring_copy(1, 1, 0).start()
+    sib_copy(0, 0).start()
+    for c2 in range(chunk, half_c):
+        fold_block(c2)
+    ring_copy(0, 1, 1).start()
+    ring_copy(1, 1, 1).start()
+    sib_copy(0, 1).start()
+
+    v_copy.wait()
+
+    @pl.loop(0, window)
+    def _(a):
+        v_folded[...] = mm(v_buf[a].reshape(bwidth * depth, width), slot_sel[...])
+        dst = pl.ds(pl.multiple_of(a * bwidth, bwidth), bwidth)
+        for c in range(depth):
+            x = v_folded[pl.ds(c, bwidth, stride=depth), :].astype(BF16)
+            c2 = c % half_c
+            v_mat[c // half_c, dst, c2 * LANES : (c2 + 1) * LANES] = x
+
+    def piece_copy(owner):
+        r = lax.rem(virt - owner + virts, virts) - 1
+        return pltpu.make_async_remote_copy(
+            src_ref=stage.at[owner],
+            dst_ref=recv.at[r],
+            send_sem=piece_send,
+            recv_sem=piece_recv,
+            device_id={"virt": owner},
+            device_id_type=MESH,
+        )
+
+    lane = iota((1, LANES), 1)
+    low = lane < pairs
+    quarter = lax.div(lane, LANES // 4)
+
+    def contract(delta):
+        k = half_c * LANES
+        block = jnp.concatenate(
+            [own[delta].reshape(k, LANES), sib[delta].reshape(k, LANES)], axis=1
+        )
+        r0 = mm(v_mat[0], block)
+        r1 = mm(v_mat[1], block)
+        keep = jnp.where(low, r0[:, :LANES], r1[:, LANES:])
+        move = jnp.where(low, r0[:, LANES:], r1[:, :LANES])
+        full = keep + pltpu.roll(move, LANES // 2, axis=1)
+        tail = ROWS - 16
+        row_own = own[delta, 0, tail:ROWS, :].astype(F32)[15:16, :]
+        row_sib = sib[delta, 0, tail:ROWS, :].astype(F32)[15:16, :]
+        row = jnp.where(low, row_own, row_sib)
+        full = jnp.where(cls_ref[...] == row, full, 0.0)
+        folded = select_dot(fold_sel[...], full)
+        far_z = lax.rem(z + delta, chips)
+        per = OUT_SLOTS // 4
+        for u in range(4):
+            piece = jnp.zeros((per, LANES), F32)
+            for q in range(4):
+                x = folded[q * per : (q + 1) * per, :]
+                shift = ((q - u) % 4) * (LANES // 4)
+                if shift:
+                    x = pltpu.roll(x, shift, axis=1)
+                piece = jnp.where(quarter == q, x, piece)
+            block_pair = far_z * CORES + (core if u < 2 else 1 - core)
+            owner = block_pair * 2 + u % 2
+            stage[owner] = piece
+
+            @pl.when(owner != virt)
+            def _():
+                piece_copy(owner).start()
+
+    def ready(delta):
+        for ch in range(2):
+            sib_copy(delta, ch).wait_recv()
+        contract(delta)
+
+    def arrive(d, ch):
+        for way in range(2):
+            if travels(way, d, ch):
+                ring_copy(way, d, ch).wait_recv()
+                if travels(way, d + 1, ch):
+                    ring_copy(way, d + 1, ch).start()
+                sib_copy((chips - d) % chips if way == 0 else d, ch).start()
+
+    arrive(1, 0)
+    ready(0)
+    arrive(1, 1)
+    for d in range(2, far):
+        arrive(d, 0)
+        ready(chips - (d - 1))
+        arrive(d, 1)
+        ready(d - 1)
+    if far > 1:
+        ready(chips - (far - 1))
+    arrive(far, 0)
+    arrive(far, 1)
+    if far > 1:
+        ready(far - 1)
+    ready(far)
+
+    pltpu.make_async_copy(recv, recv, piece_recv).wait()
+    total = stage[virt]
+    for r in range(virts - 1):
+        total = total + recv[r]
+    shifted = [total] + [pltpu.roll(total, LANES - q * (LANES // 4), axis=1) for q in (1, 2, 3)]
+    ladder = select_dot(unfold, jnp.concatenate(shifted, axis=0))
+
+    small[...] = jnp.zeros_like(small)
+    small[0:1, : oi_ref.shape[1]] = oi_ref[...].astype(F32)
+    small[1:2, : oe_ref.shape[1]] = oe_ref[...]
+    small[2:4, : po_ref.shape[1]] = po_ref[...].astype(F32)
+    orb_irr = jnp.transpose(jnp.broadcast_to(small[0:1, :], (LANES, LANES)))
+    orb_energy = jnp.transpose(jnp.broadcast_to(small[1:2, :], (LANES, LANES)))
+    orb = iota((LANES, LANES), 0)
+    hit_i = small[2:3, :].astype(jnp.int32) == orb
+    hit_j = small[3:4, :].astype(jnp.int32) == orb
+    irr_i = jnp.sum(jnp.where(hit_i, orb_irr, 0.0), axis=0, keepdims=True)
+    irr_j = jnp.sum(jnp.where(hit_j, orb_irr, 0.0), axis=0, keepdims=True)
+    energy_i = jnp.sum(jnp.where(hit_i, orb_energy, 0.0), axis=0, keepdims=True)
+    energy_j = jnp.sum(jnp.where(hit_j, orb_energy, 0.0), axis=0, keepdims=True)
+    pair_sym = jnp.bitwise_xor(irr_i.astype(jnp.int32), irr_j.astype(jnp.int32)).astype(F32)
+    denom = ((energy_i + energy_j) - energy_a) - energy_b
+    update = jnp.where(cls_ref[...] == pair_sym, ladder / denom, 0.0)
+    out_ref[...] = jnp.transpose(update)[: out_ref.shape[0], :]
+
+    for way in range(2):
+        for d in range(1, far + 1):
+            for ch in range(2):
+                if travels(way, d, ch):
+                    ring_copy(way, d, ch).wait_send()
+    for delta in range(chips):
+        for ch in range(2):
+            sib_copy(delta, ch).wait_send()
+    pltpu.make_async_copy(recv, recv, piece_send).wait()
+
+
+def folded(mesh, amplitudes, integrals, pair_occ, occ_irrep, virt_irrep, occ_energy, virt_energy):
+    chips, virts = mesh.shape["pair"] // CORES, mesh.shape["virt"]
+    pairs, depth, width = amplitudes.shape
+    window, bwidth = integrals.shape[:2]
+    abs_ = window * bwidth
+    owned = pair_occ.shape[0]
+    half_c = depth // 2
+    per = OUT_SLOTS // 4
+    vmem = pl.BlockSpec(memory_space=pltpu.VMEM)
+    hbm = pl.BlockSpec(memory_space=pl.ANY)
+    dma = pltpu.SemaphoreType.DMA
+    out = pl.pallas_call(
+        functools.partial(fold_kernel, chips, virts),
+        out_shape=jax.ShapeDtypeStruct((owned, abs_), F32),
+        in_specs=[hbm, hbm] + [vmem] * 5,
+        out_specs=vmem,
+        scratch_shapes=[
+            pltpu.VMEM(amplitudes.shape, BF16),
+            pltpu.VMEM(integrals.shape, BF16),
+            pltpu.VMEM((8, LANES), F32),
+            pltpu.VMEM((width, LANES), BF16),
+            pltpu.VMEM((width, LANES), BF16),
+            pltpu.VMEM((pairs * depth, LANES), F32),
+            pltpu.VMEM((pairs * depth, LANES), F32),
+            pltpu.VMEM((bwidth * depth, LANES), F32),
+            pltpu.VMEM((2, abs_, half_c * LANES), BF16),
+            pltpu.VMEM((abs_, LANES), F32),
+            pltpu.VMEM((OUT_SLOTS, abs_), BF16),
+            pltpu.VMEM((chips, half_c, LANES, LANES), BF16),
+            pltpu.VMEM((chips, half_c, LANES, LANES), BF16),
+            pltpu.VMEM((virts, per, LANES), F32),
+            pltpu.VMEM((virts - 1, per, LANES), F32),
+            dma((2,)),
+            dma((2, chips // 2, 2)),
+            dma((2, chips // 2, 2)),
+            dma((chips, 2)),
+            dma((chips, 2)),
+            dma,
+            dma,
+        ],
+        compiler_params=pltpu.CompilerParams(collective_id=0, has_side_effects=True),
+        name="ladder_fold",
+    )(
+        amplitudes,
+        integrals,
+        pair_occ.T,
+        occ_irrep[None, :],
+        virt_irrep[None, :],
+        occ_energy[None, :],
+        virt_energy[None, :],
+    )
+    return out.reshape(owned, window, bwidth)
+
+
+def fits(window, bwidth, virt_irrep):
+    groups = jnp.arange(IRREPS, dtype=jnp.int32)
+    hot = virt_irrep[None, :] == groups[:, None]
+    sizes = jnp.sum(hot.astype(jnp.int32), axis=1)
+    label = jnp.bitwise_xor(virt_irrep[:window, None], virt_irrep[None, :])
+    label = label.reshape(window, -1, bwidth)
+    members = jnp.sum((label[None] == groups[:, None, None, None]).astype(jnp.int32), axis=(1, 3))
+    return jnp.logical_and(jnp.max(sizes) <= CLASS_ROW, jnp.max(members) <= OUT_SLOTS)
 
 
 def table_lookup(indices, table, zero_value):
@@ -10,7 +411,7 @@
     return jnp.sum(jnp.where(hits, table[None, :], zero_value), axis=1)
 
 
-def local(amplitudes, integrals, pair_occ, occ_irrep, virt_irrep, occ_energy, virt_energy):
+def general(amplitudes, integrals, pair_occ, occ_irrep, virt_irrep, occ_energy, virt_energy):
     window_size, local_width, local_depth, full_width = integrals.shape
     integral_matrix = integrals.reshape(window_size * local_width, local_depth * full_width)
     owned_rows = pair_occ.shape[0]
@@ -48,6 +449,12 @@
 
 
 def solution(mesh):
+    def local(*args):
+        window, bwidth = args[1].shape[:2]
+        return lax.cond(
+            fits(window, bwidth, args[4]), functools.partial(folded, mesh), general, *args
+        )
+
     return jax.shard_map(
         local,
         mesh=mesh,

time: 302 us -> 63.8 us (0.21)
  the two profiles are of different devices: /device:TPU:64 before, /device:TPU:4 now
where the time goes in v1:
time: 63.8 us; the launch traced here: 63.5 us
  Pallas kernels  43.3 us (68%)
  between operations  14.7 us (23%)
  local copies, waits for them, and re-layouts  2.94 us (5%)
  other arithmetic  2.38 us (4%)
    pallas_call x1, Pallas kernels, folded(): pl.pallas_call(functools.partial(fold_kernel, chips, virts), out_shape=ja...  43.3 us

profile of v1, /device:TPU:4, one launch (start us, length us, event | category | flops | bytes accessed | tf_op | source)
XLA Modules:
  0.0 63.5 jit_solution(16945654722162785221)
XLA Ops:
  6.5 0.8 %convert_reduce_fusion.1 = s32[8]{0:T(128)S(1)} fusion(s32[512]{0:T(512)} %param.13), kind=kLoop, calls=%fused_computation.16 | loop fusion | flops 12280 | bytes 2080 | tf_op jit(solution)/shard_map/reduce_sum | solution.py:401
  7.3 0.6 %reduce_max.18 = s32[]{:T(128)} reduce(s32[8]{0:T(128)S(1)} %convert_reduce_fusion.1, s32[]{:T(128)} %constant.10.clone.1), dimensions={0}, to_apply=%region_1.0 | reduce | flops 7 | bytes 40 | tf_op jit(solution)/shard_map/reduce_max | solution.py:405
  8.6 0.8 %eq.37 = s32[16,32]{1,0:T(8,128)S(1)} reshape(s32[512]{0:T(512)} %param.13) | data formatting | bytes 4096 | tf_op jit(solution)/shard_map/eq | solution.py:400
  9.4 0.7 %slice.15 = s32[8]{0:T(128)S(1)} slice(s32[512]{0:T(512)} %param.13), slice={[0:8]} | slice | bytes 64 | tf_op jit(solution)/shard_map/slice | solution.py:402
  10.1 0.1 broadcast_xor_fusion.1
  10.1 0.2 convert_reduce_fusion
  10.4 0.6 %reduce_max.19 = s32[]{:T(128)} reduce(s32[8,16]{1,0:T(8,128)S(1)} %convert_reduce_fusion, s32[]{:T(128)} %constant.10.clone.1), dimensions={0,1}, to_apply=%region_3.0 | reduce | flops 127 | bytes 520 | tf_op jit(solution)/shard_map/reduce_max | solution.py:405
  11.7 44.3 %conditional.1 = (f32[32,8,32]{2,1,0:T(8,128)S(1)}) conditional(s32[]{:T(128)} %convert_element_type.11, (s32[32,2]{0,1:T(2,128)}, s32[120]{0:T(128)}, s32[512]{0:T(512)}, bf16[64,16,512]{2,1,0:T(8,128)(2,1)}, bf16[8,32,16,512]{3,2,1,0:T(8,128)(2,1)}, /*index=5*/f32[120]{0:T(128)}, f32[512]{0:T(512)}) %tuple.11, (s32[32,2]{0,1:T(2,128)}, ...), branch_computations={%region_4.10_spmd, %region_10.11_spmd} | conditional | flops 4295316992 | bytes 140736064 | solution.py:454
  11.9 43.3 %ladder_fold.1 = f32[32,256]{1,0:T(8,128)} custom-call(bf16[64,16,512]{2,1,0:T(8,128)(2,1)} %get-tuple-element.43.t_hbm, bf16[8,32,16,512]{3,2,1,0:T(8,128)(2,1)} %get-tuple-element.44.v_hbm, s32[2,32]{1,0:T(2,128)} %bitcast.21, s32[1,120]{1,0:T(1,128)} %bitcast.23, s32[1,512]{1,0:T(1,128)} %bitcast.20, f32[1,120]{1,0:T(1,128)} %bitcast.24, f32[1,512]{1,0:T(1,128)} %bitcast.22), custom_call_target="tpu_custom_call" | custom-call | tf_op jit(solution)/shard_map/cond/branch_1_fun/ladder_fold/pallas_call | solution.py:355
  55.1 0.8 %reshape.100 = f32[32,8,32]{2,1,0:T(8,128)S(1)} reshape(f32[32,256]{1,0:T(8,128)} %ladder_fold.1) | data formatting | bytes 65536 | tf_op jit(solution)/shard_map/cond/branch_1_fun/reshape | solution.py:395
  56.0 0.0 copy-start.1
  56.0 0.6 %copy-done.1 = f32[32,8,32]{2,1,0:T(8,128)} copy-done((f32[32,8,32]{2,1,0:T(8,128)}, f32[32,8,32]{2,1,0:T(8,128)S(1)}, u32[]{:S(2)}) %copy-start.1) | copy-done | bytes 32792
Async XLA Ops:
  56.0 0.7 %copy-start.1 = (f32[32,8,32]{2,1,0:T(8,128)}, f32[32,8,32]{2,1,0:T(8,128)S(1)}, u32[]{:S(2)}) copy-start(f32[32,8,32]{2,1,0:T(8,128)S(1)} %get-tuple-element.66) | copy-start | bytes 98308

commit v2 on v1

--- a/solution.py
+++ b/solution.py
@@ -328,7 +328,9 @@
     pair_sym = jnp.bitwise_xor(irr_i.astype(jnp.int32), irr_j.astype(jnp.int32)).astype(F32)
     denom = ((energy_i + energy_j) - energy_a) - energy_b
     update = jnp.where(cls_ref[...] == pair_sym, ladder / denom, 0.0)
-    out_ref[...] = jnp.transpose(update)[: out_ref.shape[0], :]
+    update = jnp.transpose(update)[: out_ref.shape[0], :]
+    for a in range(window):
+        out_ref[:, a, :] = update[:, a * bwidth : (a + 1) * bwidth]
 
     for way in range(2):
         for d in range(1, far + 1):
@@ -352,9 +354,9 @@
     vmem = pl.BlockSpec(memory_space=pltpu.VMEM)
     hbm = pl.BlockSpec(memory_space=pl.ANY)
     dma = pltpu.SemaphoreType.DMA
-    out = pl.pallas_call(
+    return pl.pallas_call(
         functools.partial(fold_kernel, chips, virts),
-        out_shape=jax.ShapeDtypeStruct((owned, abs_), F32),
+        out_shape=jax.ShapeDtypeStruct((owned, window, bwidth), F32),
         in_specs=[hbm, hbm] + [vmem] * 5,
         out_specs=vmem,
         scratch_shapes=[
@@ -392,17 +394,37 @@
         occ_energy[None, :],
         virt_energy[None, :],
     )
-    return out.reshape(owned, window, bwidth)
+
+
+def fits_kernel(window, bwidth, vi_ref, out_ref):
+    width = vi_ref.shape[1]
+    vi = vi_ref[...]
+    group = iota((IRREPS, width), 0)
+    sizes = jnp.sum(jnp.where(vi == group, 1.0, 0.0), axis=1, keepdims=True)
+    lane = iota((window, width), 1)
+    irr_a = jnp.sum(
+        jnp.where(lane == iota((window, width), 0), vi.astype(F32), 0.0), axis=1, keepdims=True
+    )
+    label = jnp.bitwise_xor(irr_a.astype(jnp.int32), vi)
+    per_b = [
+        jnp.sum(jnp.where(label == g, 1.0, 0.0), axis=0, keepdims=True) for g in range(IRREPS)
+    ]
+    per_b = jnp.concatenate(per_b, axis=0).astype(BF16)
+    blocks = iota((width, LANES), 1) == lax.div(iota((width, LANES), 0), bwidth)
+    members = mm(per_b, jnp.where(blocks, 1.0, 0.0).astype(BF16))
+    fit = jnp.logical_and(jnp.max(sizes) <= CLASS_ROW, jnp.max(members) <= OUT_SLOTS)
+    out_ref[0, 0] = jnp.where(fit, 1, 0)
 
 
 def fits(window, bwidth, virt_irrep):
-    groups = jnp.arange(IRREPS, dtype=jnp.int32)
-    hot = virt_irrep[None, :] == groups[:, None]
-    sizes = jnp.sum(hot.astype(jnp.int32), axis=1)
-    label = jnp.bitwise_xor(virt_irrep[:window, None], virt_irrep[None, :])
-    label = label.reshape(window, -1, bwidth)
-    members = jnp.sum((label[None] == groups[:, None, None, None]).astype(jnp.int32), axis=(1, 3))
-    return jnp.logical_and(jnp.max(sizes) <= CLASS_ROW, jnp.max(members) <= OUT_SLOTS)
+    flag = pl.pallas_call(
+        functools.partial(fits_kernel, window, bwidth),
+        out_shape=jax.ShapeDtypeStruct((1, 1), jnp.int32),
+        in_specs=[pl.BlockSpec(memory_space=pltpu.VMEM)],
+        out_specs=pl.BlockSpec(memory_space=pltpu.SMEM),
+        name="fits",
+    )(virt_irrep[None, :])
+    return flag[0, 0] > 0
 
 
 def table_lookup(indices, table, zero_value):
@@ -415,13 +437,41 @@
     window_size, local_width, local_depth, full_width = integrals.shape
     integral_matrix = integrals.reshape(window_size * local_width, local_depth * full_width)
     owned_rows = pair_occ.shape[0]
-    block_rows = lax.all_gather(amplitudes, "pair", axis=0, tiled=True)
-    flattened = block_rows.reshape(block_rows.shape[0], local_depth * full_width)
-    partial_value = lax.dot_general(
-        flattened, integral_matrix, (((1,), (1,)), ((), ())), preferred_element_type=jnp.float32
-    )
-    summed = lax.psum(partial_value, "virt")
-    ladder = lax.dynamic_slice_in_dim(summed, lax.axis_index("virt") * owned_rows, owned_rows, 0)
+    block = amplitudes.shape[0]
+    blocks, owners = lax.axis_size("pair"), lax.axis_size("virt")
+    here, owner = lax.axis_index("pair"), lax.axis_index("virt")
+
+    ring = [(i, (i + 1) % blocks) for i in range(blocks)]
+
+    def multiply(step, held, partial_value):
+        rows = lax.dot_general(
+            held.reshape(block, local_depth * full_width),
+            integral_matrix,
+            (((1,), (1,)), ((), ())),
+            preferred_element_type=jnp.float32,
+        )
+        first = lax.rem(here - step + blocks, blocks) * block
+        return lax.dynamic_update_slice_in_dim(partial_value, rows, first, 0)
+
+    def hop(step, carry):
+        held, partial_value = carry
+        return lax.ppermute(held, "pair", ring), multiply(step, held, partial_value)
+
+    empty = jnp.zeros((block * blocks, integral_matrix.shape[0]), jnp.float32)
+    first_hop = hop(0, (amplitudes, empty))
+    held, partial_value = lax.fori_loop(1, blocks - 1, hop, first_hop)
+    partial_value = multiply(blocks - 1, held, partial_value)
+
+    def term(step):
+        first = lax.rem(owner - 1 - step + 2 * owners, owners) * owned_rows
+        return lax.dynamic_slice_in_dim(partial_value, first, owned_rows, 0)
+
+    owner_ring = [(i, (i + 1) % owners) for i in range(owners)]
+
+    def reduce(step, total):
+        return lax.ppermute(total, "virt", owner_ring) + term(step)
+
+    ladder = lax.fori_loop(1, owners, reduce, term(0))
     ladder = ladder.reshape(owned_rows, window_size, local_width)
     b_offset = lax.axis_index("pair") * local_width
     local_sym = lax.dynamic_slice_in_dim(virt_irrep, b_offset, local_width, 0)

time: 63.8 us -> 46.1 us (0.72)
  between operations: 14.7 us -> 0.67 us
  other arithmetic: 2.38 us -> 0 us
  local copies, waits for them, and re-layouts: 2.94 us -> 0.66 us
  Pallas kernels: 43.3 us -> 44.5 us
    pallas_call x0 -> x1, Pallas kernels: none -> 1.56 us  [fits(): pl.pallas_call(functools.partial(fits_kernel, window, bwidth), out_shape=...]
    reduce_max x2 -> x0, other arithmetic: 1.28 us -> none  [the longest x1 0.64 us: fits(): jnp.max(members) <= OUT_SLOTS]
    reduce_sum x2 -> x0, other arithmetic: 1.03 us -> none  [the longest x1 0.8 us: fits(): sizes = jnp.sum(hot.astype(jnp.int32), axis=1)]
    reshape x1 -> x0, local copies, waits for them, and re-layouts: 0.84 us -> none  [folded(): return out.reshape(owned, window, bwidth)]
    eq x1 -> x0, local copies, waits for them, and re-layouts: 0.76 us -> none  [fits(): hot = virt_irrep[None, :] == groups[:, None]]
    slice x1 -> x0, local copies, waits for them, and re-layouts: 0.68 us -> none  [fits(): label = jnp.bitwise_xor(virt_irrep[:window, None], virt_irrep[None, :])]
where the time goes in v2:
time: 46.1 us; the launch traced here: 46 us
  Pallas kernels  44.5 us (97%)
  between operations  0.67 us (1%)
  local copies, waits for them, and re-layouts  0.66 us (1%)
    pallas_call x1, Pallas kernels, folded(): pl.pallas_call(functools.partial(fold_kernel, chips, virts), out_shape=ja...  42.9 us
    pallas_call x1, Pallas kernels, fits(): pl.pallas_call(functools.partial(fits_kernel, window, bwidth), out_shape=...  1.56 us

profile of v2, /device:TPU:4, one launch (start us, length us, event | category | flops | bytes accessed | tf_op | source)
XLA Modules:
  0.0 46.0 jit_solution(8862687424041746788)
XLA Ops:
  0.0 1.6 %fits.1 = s32[1,1]{1,0:T(1,128)} custom-call(s32[1,512]{1,0:T(1,128)} %bitcast.43), custom_call_target="tpu_custom_call" | custom-call | tf_op jit(solution)/shard_map/fits/pallas_call | solution.py:420
  2.2 43.1 %conditional.1 = (f32[32,8,32]{2,1,0:T(8,128)S(1)}) conditional(s32[]{:T(128)} %bitcast.8, (s32[32,2]{0,1:T(2,128)}, s32[120]{0:T(128)}, s32[512]{0:T(512)}, bf16[64,16,512]{2,1,0:T(8,128)(2,1)}, bf16[8,32,16,512]{3,2,1,0:T(8,128)(2,1)}, /*index=5*/f32[120]{0:T(128)}, f32[512]{0:T(512)}) %tuple.46, (s32[32,2]{0,1:T(2,128)}, s32[120]{0:T(128)}, ...), branch_computations={%region_0.9_spmd, %region_9.10_spmd} | conditional | flops 805402112 | bytes 46774768 | solution.py:504
  2.4 42.9 %ladder_fold.1 = f32[32,8,32]{2,1,0:T(8,128)S(1)} custom-call(bf16[64,16,512]{2,1,0:T(8,128)(2,1)} %get-tuple-element.246.t_hbm, bf16[8,32,16,512]{3,2,1,0:T(8,128)(2,1)} %get-tuple-element.247.v_hbm, s32[2,32]{1,0:T(2,128)} %bitcast.45, s32[1,120]{1,0:T(1,128)} %bitcast.47, s32[1,512]{1,0:T(1,128)} %bitcast.44, f32[1,120]{1,0:T(1,128)} %bitcast.48, ...), custom_call_target="tpu_custom_call" | custom-call | tf_op jit(solution)/shard_map/cond/branch_1_fun/ladder_fold/pallas_call | solution.py:357
  45.3 0.7 %copy.37 = f32[32,8,32]{2,1,0:T(8,128)} copy(f32[32,8,32]{2,1,0:T(8,128)S(1)} %get-tuple-element.253) | data formatting | bytes 65536

commit v3 on v2

--- a/solution.py
+++ b/solution.py
@@ -13,8 +13,8 @@
 
 IRREPS = 8
 LANES = 128
-ROWS = 96
-CLASS_ROW = ROWS - 1
+ROWS = (80, 96)
+CHUNKS = 4
 OUT_SLOTS = 64
 CORES = 2
 
@@ -43,6 +43,7 @@
 def fold_kernel(
     chips,
     virts,
+    rows_sent,
     t_hbm,
     v_hbm,
     po_ref,
@@ -60,17 +61,17 @@
     t_seen,
     v_folded,
     v_mat,
+    v_other,
     cls_ref,
     fold_sel,
-    own,
-    sib,
+    gathered,
     stage,
     recv,
     local_sem,
     ring_send,
     ring_recv,
-    sib_send,
-    sib_recv,
+    swap_send,
+    swap_recv,
     piece_send,
     piece_recv,
 ):
@@ -78,7 +79,8 @@
     window, bwidth = v_buf.shape[0], v_buf.shape[1]
     abs_ = window * bwidth
     half_c = depth // 2
-    chunk = half_c // 2
+    chunk = half_c // CHUNKS
+    class_row = rows_sent - 1
 
     pair = lax.axis_index("pair")
     virt = lax.axis_index("virt")
@@ -87,6 +89,9 @@
     up = lax.rem(z + 1, chips) * CORES + core
     down = lax.rem(z + chips - 1, chips) * CORES + core
     other = z * CORES + (1 - core)
+    source_core = lax.rem(lax.div(virt, 2), CORES)
+    keeps_one = source_core == core
+    kept = jnp.where(keeps_one, 1, 0)
 
     t_copy = pltpu.make_async_copy(t_hbm, t_buf, local_sem.at[0])
     v_copy = pltpu.make_async_copy(v_hbm, v_buf, local_sem.at[1])
@@ -97,13 +102,20 @@
     for q in (up, down, other):
         pl.semaphore_signal(barrier, inc=1, device_id={"pair": q}, device_id_type=MESH)
 
-    @pl.loop(1, virts)
+    @pl.loop(0, virts)
     def _(k):
         w = lax.rem(virt + k, virts)
-        pl.semaphore_signal(barrier, inc=1, device_id={"virt": w}, device_id_type=MESH)
-
-    for blocks in (own, sib):
-        blocks[:, :, ROWS:, :] = jnp.zeros((chips, half_c, LANES - ROWS, LANES), BF16)
+
+        @pl.when(jnp.logical_or(w != virt, jnp.logical_not(keeps_one)))
+        def _():
+            pl.semaphore_signal(
+                barrier,
+                inc=1,
+                device_id={"pair": z * CORES + source_core, "virt": w},
+                device_id_type=MESH,
+            )
+
+    gathered[:, :, rows_sent:, :] = jnp.zeros((chips, half_c, LANES - rows_sent, LANES), BF16)
 
     vi = vi_ref[...].astype(F32)
     ve = ve_ref[...]
@@ -127,27 +139,6 @@
         lane_s < IRREPS, jnp.bitwise_xor(irr_c.astype(jnp.int32), lane_s), 0
     ).astype(F32)
 
-    lane_ab = iota((abs_, width), 1)
-    sub_ab = iota((abs_, width), 0)
-    sub_a = lax.div(sub_ab, bwidth)
-    hit_a = lane_ab == sub_a
-    hit_b = lane_ab == pair * bwidth + (sub_ab - sub_a * bwidth)
-    irr_a = jnp.sum(jnp.where(hit_a, vi, 0.0), axis=1, keepdims=True)
-    irr_b = jnp.sum(jnp.where(hit_b, vi, 0.0), axis=1, keepdims=True)
-    energy_a = jnp.sum(jnp.where(hit_a, ve, 0.0), axis=1, keepdims=True)
-    energy_b = jnp.sum(jnp.where(hit_b, ve, 0.0), axis=1, keepdims=True)
-    cls = jnp.bitwise_xor(irr_a.astype(jnp.int32), irr_b.astype(jnp.int32))
-    lane_k = iota((abs_, LANES), 1)
-    hot_ab = cls == lane_k
-    hot_ab_f = jnp.where(hot_ab, 1.0, 0.0)
-    before = jnp.where(iota((abs_, abs_), 1) < iota((abs_, abs_), 0), 1.0, 0.0).astype(BF16)
-    ranks = jnp.where(hot_ab, mm(before, hot_ab_f.astype(BF16)), 0.0)
-    rank = jnp.sum(ranks, axis=1, keepdims=True).astype(jnp.int32)
-    unfold_f = jnp.where(rank == lane_k, 1.0, 0.0)
-    unfold = unfold_f.astype(BF16)[:, :OUT_SLOTS]
-    fold_sel[...] = jnp.transpose(unfold_f)[:OUT_SLOTS, :].astype(BF16)
-    cls_ref[...] = jnp.broadcast_to(cls.astype(F32), (abs_, LANES))
-
     t_copy.wait()
     rows = pairs * depth
     t_rows = t_buf[...].reshape(rows, width)
@@ -170,51 +161,35 @@
         )
         if c2 == 0:
             label = jnp.concatenate([pair_cls, pair_cls], axis=0)
-            x = jnp.where(iota(x.shape, 1) == CLASS_ROW, label, x)
-        own[0, c2, :ROWS, :] = jnp.transpose(x)[:ROWS, :].astype(BF16)
-
-    def part(blocks, delta, ch):
-        return blocks.at[delta, pl.ds(ch * chunk, chunk), pl.ds(0, ROWS), :]
+            x = jnp.where(iota(x.shape, 1) == class_row, label, x)
+        gathered[0, c2, :rows_sent, :] = jnp.transpose(x)[:rows_sent, :].astype(BF16)
 
     def ring_copy(way, d, ch):
         src, dst = d - 1, d
         if way == 0:
             src, dst = (chips - src) % chips, (chips - dst) % chips
+        part = (pl.ds(ch * chunk, chunk), pl.ds(0, rows_sent))
         return pltpu.make_async_remote_copy(
-            src_ref=part(own, src, ch),
-            dst_ref=part(own, dst, ch),
+            src_ref=gathered.at[src, part[0], part[1], :],
+            dst_ref=gathered.at[dst, part[0], part[1], :],
             send_sem=ring_send.at[way, d - 1, ch],
             recv_sem=ring_recv.at[way, d - 1, ch],
             device_id={"pair": up if way == 0 else down},
             device_id_type=MESH,
         )
 
-    def sib_copy(delta, ch):
-        return pltpu.make_async_remote_copy(
-            src_ref=part(own, delta, ch),
-            dst_ref=part(sib, delta, ch),
-            send_sem=sib_send.at[delta, ch],
-            recv_sem=sib_recv.at[delta, ch],
-            device_id={"pair": other},
-            device_id_type=MESH,
-        )
-
     far = chips // 2
 
     def travels(way, d, ch):
-        return d < far or (d == far and ch == way)
-
-    for c2 in range(chunk):
+        return d < far or (d == far and ch // (CHUNKS // 2) == way)
+
+    for c2 in range(half_c):
         fold_block(c2)
-    pl.semaphore_wait(barrier, virts - 1 + 3)
-    ring_copy(0, 1, 0).start()
-    ring_copy(1, 1, 0).start()
-    sib_copy(0, 0).start()
-    for c2 in range(chunk, half_c):
-        fold_block(c2)
-    ring_copy(0, 1, 1).start()
-    ring_copy(1, 1, 1).start()
-    sib_copy(0, 1).start()
+        if c2 == chunk - 1:
+            pl.semaphore_wait(barrier, virts + 3 - kept)
+        if (c2 + 1) % chunk == 0:
+            for way in range(2):
+                ring_copy(way, 1, c2 // chunk).start()
 
     v_copy.wait()
 
@@ -227,14 +202,48 @@
             c2 = c % half_c
             v_mat[c // half_c, dst, c2 * LANES : (c2 + 1) * LANES] = x
 
-    def piece_copy(owner):
-        r = lax.rem(virt - owner + virts, virts) - 1
+    swap = pltpu.make_async_remote_copy(
+        src_ref=v_mat,
+        dst_ref=v_other,
+        send_sem=swap_send,
+        recv_sem=swap_recv,
+        device_id={"pair": other},
+        device_id_type=MESH,
+    )
+    swap.start()
+
+    lane_ab = iota((abs_, width), 1)
+    sub_ab = iota((abs_, width), 0)
+    sub_a = lax.div(sub_ab, bwidth)
+    sub_b = sub_ab - sub_a * bwidth
+    hit_a = lane_ab == sub_a
+    irr_a = jnp.sum(jnp.where(hit_a, vi, 0.0), axis=1, keepdims=True).astype(jnp.int32)
+    lane_k = iota((abs_, LANES), 1)
+    before = jnp.where(iota((abs_, abs_), 1) < iota((abs_, abs_), 0), 1.0, 0.0).astype(BF16)
+    unfold = None
+    for k, q in enumerate((pair, other)):
+        hit_b = lane_ab == q * bwidth + sub_b
+        irr_b = jnp.sum(jnp.where(hit_b, vi, 0.0), axis=1, keepdims=True).astype(jnp.int32)
+        cls = jnp.bitwise_xor(irr_a, irr_b)
+        hot_ab = cls == lane_k
+        hot_ab_f = jnp.where(hot_ab, 1.0, 0.0)
+        ranks = jnp.where(hot_ab, mm(before, hot_ab_f.astype(BF16)), 0.0)
+        rank = jnp.sum(ranks, axis=1, keepdims=True).astype(jnp.int32)
+        unfold_f = jnp.where(rank == lane_k, 1.0, 0.0)
+        if k == 0:
+            unfold = unfold_f.astype(BF16)[:, :OUT_SLOTS]
+            energy_a = jnp.sum(jnp.where(hit_a, ve, 0.0), axis=1, keepdims=True)
+            energy_b = jnp.sum(jnp.where(hit_b, ve, 0.0), axis=1, keepdims=True)
+        fold_sel[k] = jnp.transpose(unfold_f)[:OUT_SLOTS, :].astype(BF16)
+        cls_ref[k] = jnp.broadcast_to(cls.astype(F32), (abs_, LANES))
+
+    def piece_copy(k, index, owner):
         return pltpu.make_async_remote_copy(
-            src_ref=stage.at[owner],
-            dst_ref=recv.at[r],
+            src_ref=stage.at[k, index],
+            dst_ref=recv.at[virt],
             send_sem=piece_send,
             recv_sem=piece_recv,
-            device_id={"virt": owner},
+            device_id={"pair": other if k else pair, "virt": owner},
             device_id_type=MESH,
         )
 
@@ -242,25 +251,28 @@
     low = lane < pairs
     quarter = lax.div(lane, LANES // 4)
 
-    def contract(delta):
-        k = half_c * LANES
-        block = jnp.concatenate(
-            [own[delta].reshape(k, LANES), sib[delta].reshape(k, LANES)], axis=1
-        )
-        r0 = mm(v_mat[0], block)
-        r1 = mm(v_mat[1], block)
-        keep = jnp.where(low, r0[:, :LANES], r1[:, LANES:])
-        move = jnp.where(low, r0[:, LANES:], r1[:, :LANES])
+    def class_of(delta):
+        tail = rows_sent - 16
+        return gathered[delta, 0, tail:rows_sent, :].astype(F32)[15:16, :]
+
+    def contract(k, deltas):
+        depth_k = half_c * LANES
+        blocks = [gathered[delta].reshape(depth_k, LANES) for delta in deltas]
+        block = jnp.concatenate(blocks, axis=1) if len(blocks) > 1 else blocks[0]
+        mat = v_other if k else v_mat
+        r0 = mm(mat[0], block)
+        r1 = mm(mat[1], block)
+        if len(deltas) > 1:
+            keep = jnp.where(low, r0[:, :LANES], r1[:, LANES:])
+            move = jnp.where(low, r0[:, LANES:], r1[:, :LANES])
+            row = jnp.where(low, class_of(deltas[0]), class_of(deltas[1]))
+        else:
+            keep, move, row = r0, r1, class_of(deltas[0])
         full = keep + pltpu.roll(move, LANES // 2, axis=1)
-        tail = ROWS - 16
-        row_own = own[delta, 0, tail:ROWS, :].astype(F32)[15:16, :]
-        row_sib = sib[delta, 0, tail:ROWS, :].astype(F32)[15:16, :]
-        row = jnp.where(low, row_own, row_sib)
-        full = jnp.where(cls_ref[...] == row, full, 0.0)
-        folded = select_dot(fold_sel[...], full)
-        far_z = lax.rem(z + delta, chips)
+        full = jnp.where(cls_ref[k] == row, full, 0.0)
+        folded = select_dot(fold_sel[k], full)
         per = OUT_SLOTS // 4
-        for u in range(4):
+        for u in range(2 * len(deltas)):
             piece = jnp.zeros((per, LANES), F32)
             for q in range(4):
                 x = folded[q * per : (q + 1) * per, :]
@@ -268,18 +280,21 @@
                 if shift:
                     x = pltpu.roll(x, shift, axis=1)
                 piece = jnp.where(quarter == q, x, piece)
-            block_pair = far_z * CORES + (core if u < 2 else 1 - core)
-            owner = block_pair * 2 + u % 2
-            stage[owner] = piece
-
-            @pl.when(owner != virt)
-            def _():
-                piece_copy(owner).start()
-
-    def ready(delta):
-        for ch in range(2):
-            sib_copy(delta, ch).wait_recv()
-        contract(delta)
+            delta, half = deltas[u // 2], u % 2
+            owner = (lax.rem(z + delta, chips) * CORES + core) * 2 + half
+            index = delta * 2 + half
+            stage[k, index] = piece
+            if k:
+                piece_copy(k, index, owner).start()
+            else:
+
+                @pl.when(owner != virt)
+                def _():
+                    piece_copy(k, index, owner).start()
+
+                @pl.when(owner == virt)
+                def _():
+                    recv[virt] = piece
 
     def arrive(d, ch):
         for way in range(2):
@@ -287,28 +302,33 @@
                 ring_copy(way, d, ch).wait_recv()
                 if travels(way, d + 1, ch):
                     ring_copy(way, d + 1, ch).start()
-                sib_copy((chips - d) % chips if way == 0 else d, ch).start()
-
-    arrive(1, 0)
-    ready(0)
-    arrive(1, 1)
-    for d in range(2, far):
-        arrive(d, 0)
-        ready(chips - (d - 1))
-        arrive(d, 1)
-        ready(d - 1)
-    if far > 1:
-        ready(chips - (far - 1))
-    arrive(far, 0)
-    arrive(far, 1)
-    if far > 1:
-        ready(far - 1)
-    ready(far)
-
-    pltpu.make_async_copy(recv, recv, piece_recv).wait()
-    total = stage[virt]
-    for r in range(virts - 1):
-        total = total + recv[r]
+
+    todo = [(0, (0,)), (1, (0,))]
+    swapped = False
+    for d in range(1, far + 1):
+        for ch in range(CHUNKS):
+            arrive(d, ch)
+            if todo:
+                k, deltas = todo.pop(0)
+                if k and not swapped:
+                    swap.wait_recv()
+                    swapped = True
+                contract(k, deltas)
+        deltas = (d, chips - d) if d < far else (far,)
+        todo += [(0, deltas), (1, deltas)]
+    for k, deltas in todo:
+        contract(k, deltas)
+
+    for held in range(2):
+
+        @pl.when(kept == held)
+        def _():
+            part = recv.at[pl.ds(0, virts - held)]
+            pltpu.make_async_copy(part, part, piece_recv).wait()
+
+    total = recv[0]
+    for w in range(1, virts):
+        total = total + recv[w]
     shifted = [total] + [pltpu.roll(total, LANES - q * (LANES // 4), axis=1) for q in (1, 2, 3)]
     ladder = select_dot(unfold, jnp.concatenate(shifted, axis=0))
 
@@ -327,23 +347,36 @@
     energy_j = jnp.sum(jnp.where(hit_j, orb_energy, 0.0), axis=0, keepdims=True)
     pair_sym = jnp.bitwise_xor(irr_i.astype(jnp.int32), irr_j.astype(jnp.int32)).astype(F32)
     denom = ((energy_i + energy_j) - energy_a) - energy_b
-    update = jnp.where(cls_ref[...] == pair_sym, ladder / denom, 0.0)
+    update = jnp.where(cls_ref[0] == pair_sym, ladder / denom, 0.0)
     update = jnp.transpose(update)[: out_ref.shape[0], :]
     for a in range(window):
         out_ref[:, a, :] = update[:, a * bwidth : (a + 1) * bwidth]
 
     for way in range(2):
         for d in range(1, far + 1):
-            for ch in range(2):
+            for ch in range(CHUNKS):
                 if travels(way, d, ch):
                     ring_copy(way, d, ch).wait_send()
-    for delta in range(chips):
-        for ch in range(2):
-            sib_copy(delta, ch).wait_send()
-    pltpu.make_async_copy(recv, recv, piece_send).wait()
-
-
-def folded(mesh, amplitudes, integrals, pair_occ, occ_irrep, virt_irrep, occ_energy, virt_energy):
+    swap.wait_send()
+    for held in range(2):
+
+        @pl.when(kept == held)
+        def _():
+            part = recv.at[pl.ds(0, virts - held)]
+            pltpu.make_async_copy(part, part, piece_send).wait()
+
+
+def folded(
+    mesh,
+    rows_sent,
+    amplitudes,
+    integrals,
+    pair_occ,
+    occ_irrep,
+    virt_irrep,
+    occ_energy,
+    virt_energy,
+):
     chips, virts = mesh.shape["pair"] // CORES, mesh.shape["virt"]
     pairs, depth, width = amplitudes.shape
     window, bwidth = integrals.shape[:2]
@@ -355,7 +388,7 @@
     hbm = pl.BlockSpec(memory_space=pl.ANY)
     dma = pltpu.SemaphoreType.DMA
     return pl.pallas_call(
-        functools.partial(fold_kernel, chips, virts),
+        functools.partial(fold_kernel, chips, virts, rows_sent),
         out_shape=jax.ShapeDtypeStruct((owned, window, bwidth), F32),
         in_specs=[hbm, hbm] + [vmem] * 5,
         out_specs=vmem,
@@ -369,22 +402,22 @@
             pltpu.VMEM((pairs * depth, LANES), F32),
             pltpu.VMEM((bwidth * depth, LANES), F32),
             pltpu.VMEM((2, abs_, half_c * LANES), BF16),
-            pltpu.VMEM((abs_, LANES), F32),
-            pltpu.VMEM((OUT_SLOTS, abs_), BF16),
+            pltpu.VMEM((2, abs_, half_c * LANES), BF16),
+            pltpu.VMEM((2, abs_, LANES), F32),
+            pltpu.VMEM((2, OUT_SLOTS, abs_), BF16),
             pltpu.VMEM((chips, half_c, LANES, LANES), BF16),
-            pltpu.VMEM((chips, half_c, LANES, LANES), BF16),
+            pltpu.VMEM((2, 2 * chips, per, LANES), F32),
             pltpu.VMEM((virts, per, LANES), F32),
-            pltpu.VMEM((virts - 1, per, LANES), F32),
             dma((2,)),
-            dma((2, chips // 2, 2)),
-            dma((2, chips // 2, 2)),
-            dma((chips, 2)),
-            dma((chips, 2)),
+            dma((2, chips // 2, CHUNKS)),
+            dma((2, chips // 2, CHUNKS)),
+            dma,
+            dma,
             dma,
             dma,
         ],
-        compiler_params=pltpu.CompilerParams(collective_id=0, has_side_effects=True),
-        name="ladder_fold",
+        compiler_params=pltpu.CompilerParams(collective_id=rows_sent, has_side_effects=True),
+        name=f"ladder_fold_{rows_sent}",
     )(
         amplitudes,
         integrals,
@@ -412,19 +445,22 @@
     per_b = jnp.concatenate(per_b, axis=0).astype(BF16)
     blocks = iota((width, LANES), 1) == lax.div(iota((width, LANES), 0), bwidth)
     members = mm(per_b, jnp.where(blocks, 1.0, 0.0).astype(BF16))
-    fit = jnp.logical_and(jnp.max(sizes) <= CLASS_ROW, jnp.max(members) <= OUT_SLOTS)
-    out_ref[0, 0] = jnp.where(fit, 1, 0)
+    largest = jnp.max(sizes)
+    case = 0
+    for rows in ROWS:
+        case += jnp.where(largest <= rows - 1, 0, 1)
+    out_ref[0, 0] = jnp.where(jnp.max(members) <= OUT_SLOTS, case, len(ROWS))
 
 
 def fits(window, bwidth, virt_irrep):
-    flag = pl.pallas_call(
+    case = pl.pallas_call(
         functools.partial(fits_kernel, window, bwidth),
         out_shape=jax.ShapeDtypeStruct((1, 1), jnp.int32),
         in_specs=[pl.BlockSpec(memory_space=pltpu.VMEM)],
         out_specs=pl.BlockSpec(memory_space=pltpu.SMEM),
         name="fits",
     )(virt_irrep[None, :])
-    return flag[0, 0] > 0
+    return case[0, 0]
 
 
 def table_lookup(indices, table, zero_value):
@@ -501,9 +537,8 @@
 def solution(mesh):
     def local(*args):
         window, bwidth = args[1].shape[:2]
-        return lax.cond(
-            fits(window, bwidth, args[4]), functools.partial(folded, mesh), general, *args
-        )
+        branches = [functools.partial(folded, mesh, rows) for rows in ROWS] + [general]
+        return lax.switch(fits(window, bwidth, args[4]), branches, *args)
 
     return jax.shard_map(
         local,

time: 46.1 us -> 43.2 us (0.937); the launches traced: 46 us -> 42.5 us
  Pallas kernels: 44.5 us -> 41 us
    pallas_call x1, Pallas kernels: 42.9 us -> 39.4 us  [folded(): pl.pallas_call(functools.partial(fold_kernel, chips, virts, rows_sent), o...]
where the time goes in v3:
time: 43.2 us; the launch traced here: 42.5 us
  Pallas kernels  41 us (95%)
  between operations  0.67 us (2%)
  local copies, waits for them, and re-layouts  0.66 us (2%)
    pallas_call x1, Pallas kernels, folded(): pl.pallas_call(functools.partial(fold_kernel, chips, virts, rows_sent), o...  39.4 us
    pallas_call x1, Pallas kernels, fits(): pl.pallas_call(functools.partial(fits_kernel, window, bwidth), out_shape=...  1.55 us

profile of v3, /device:TPU:4, one launch (start us, length us, event | category | flops | bytes accessed | tf_op | source)
XLA Modules:
  0.0 42.5 jit_solution(13287838275134098602)
XLA Ops:
  0.0 1.6 %fits.1 = s32[1,1]{1,0:T(1,128)} custom-call(s32[1,512]{1,0:T(1,128)} %bitcast.48), custom_call_target="tpu_custom_call" | custom-call | tf_op jit(solution)/shard_map/fits/pallas_call | solution.py:456
  2.2 39.6 %conditional.1 = (f32[32,8,32]{2,1,0:T(8,128)S(1)}) conditional(s32[]{:T(128)} %bitcast.13, (s32[32,2]{0,1:T(2,128)}, s32[120]{0:T(128)}, s32[512]{0:T(512)}, f32[120]{0:T(128)}, f32[512]{0:T(512)}, /*index=5*/bf16[64,16,512]{2,1,0:T(8,128)(2,1)}, bf16[8,32,16,512]{3,2,1,0:T(8,128)(2,1)}) %tuple.49, (s32[32,2]{0,1:T(2,128)}, ...), branch_computations={%region_0.0_spmd, %region_1.0_spmd, %region_2.11_spmd} | conditional | flops 805402112 | bytes 50969104 | solution.py:541
  2.2 39.4 %ladder_fold_80.1 = f32[32,8,32]{2,1,0:T(8,128)S(1)} custom-call(bf16[64,16,512]{2,1,0:T(8,128)(2,1)} %get-tuple-element.240.t_hbm, bf16[8,32,16,512]{3,2,1,0:T(8,128)(2,1)} %get-tuple-element.241.v_hbm, s32[2,32]{1,0:T(2,128)} %bitcast.51, s32[1,120]{1,0:T(1,128)} %bitcast.55, s32[1,512]{1,0:T(1,128)} %bitcast.49, f32[1,120]{1,0:T(1,128)} %bitcast.57, ...), custom_call_target="tpu_custom_call" | custom-call | tf_op jit(solution)/shard_map/cond/branch_0_fun/ladder_fold_80/pallas_call | solution.py:390
  41.9 0.7 %copy.39 = f32[32,8,32]{2,1,0:T(8,128)} copy(f32[32,8,32]{2,1,0:T(8,128)S(1)} %get-tuple-element.275) | data formatting | bytes 65536
